TPU v7x, 128 devices: a whole 4x4x4 slice. The times are simulated.
128 devices in a mesh: mesh: 16 (over z, x), bg: 8 (over y, core).
Axes of the slice: x: 4, y: 4, z: 4, core: 2. Of those that a mesh axis runs over, the one named last changes fastest.
Arguments:
- displacement: float32 [3, 64, 32, 128], P(None, 'mesh', 'bg'), may hold values from -0.4 to 0.4
- bg_coef: float32 [8, 2097152], P(None, ('mesh', 'bg')), may hold values from -0.3 to 0.3
- query_elem: int32 [128, 128, 136], P(('mesh', 'bg')), may hold values from 0 to 16383
- query_point: int32 [128, 128, 136], P(('mesh', 'bg')), may hold values from 0 to 6912, as said below
- query_coord: float32 [128, 128, 3, 136], P(('mesh', 'bg')), may hold values from 0 to 1
Outputs:
- new_displacement: float32 [3, 64, 32, 128], P(None, 'mesh', 'bg')
- line_coeffs: float32 [2, 5], replicated
Inputs may be any that keep to these rules, and one draw needn't show every extreme that they name: `query_point`: in each row every quadrature point 0 to 6911 of the row's device fills exactly one slot; all other slots hold 6912 and are empty. In every draw some owner's bucket is full in every row.
All inputs are finite; a program needn't handle non-finite values.
Results may differ from a plain program's by a relative error of at most 0.0003.
Values sent between devices are 32-bit elements; how exact they have to be, the bound alone decides.
No kernel may reach another device: no remote copies, remote signals or barrier semaphores. Data moves between devices by JAX's collectives and lax.ppermute only.
A program may use at most 64 MiB of HBM per device.

v0:
```python
import jax
import jax.numpy as jnp
import numpy as np
from jax import lax
from jax.sharding import PartitionSpec as P

PASSES = 2
LS_STEPS = 4
GAUSS_POINTS = np.array([0.5 - 0.5 * np.sqrt(0.6), 0.5, 0.5 + 0.5 * np.sqrt(0.6)])
GAUSS_WEIGHTS = np.array([5.0 / 18.0, 8.0 / 18.0, 5.0 / 18.0])


def extended(block, sides, width):
    for axis, dim in sides:
        count = lax.axis_size(axis)
        forward = [(i, i + 1) for i in range(count - 1)]
        forward.append((count - 1, 0))
        backward = [(target, source) for source, target in forward]
        low = lax.ppermute(
            lax.slice_in_dim(block, block.shape[dim] - width, None, axis=dim), axis, forward
        )
        high = lax.ppermute(lax.slice_in_dim(block, 0, width, axis=dim), axis, backward)
        block = jnp.concatenate([low, block, high], axis=dim)
    return block


def basis_tables(elements, periodic):
    node_count = 2 * elements if periodic else 2 * elements + 1
    values = np.zeros((node_count, 3 * elements))
    slopes = np.zeros((node_count, 3 * elements))
    points = GAUSS_POINTS
    shape_values = [
        2.0 * (points - 0.5) * (points - 1.0),
        -4.0 * points * (points - 1.0),
        2.0 * points * (points - 0.5),
    ]
    shape_slopes = [4.0 * points - 3.0, 4.0 - 8.0 * points, 4.0 * points - 1.0]
    for offset in range(3):
        node_rows = (2 * np.arange(elements) + offset) % node_count
        for gauss_index in range(3):
            columns = 3 * np.arange(elements) + gauss_index
            values[node_rows, columns] += shape_values[offset][gauss_index]
            slopes[node_rows, columns] += shape_slopes[offset][gauss_index]
    return (jnp.asarray(values, dtype=jnp.float32), jnp.asarray(slopes, dtype=jnp.float32))


def quad_weights(z_elems, y_elems, x_elems):
    along_z = jnp.asarray(np.tile(GAUSS_WEIGHTS, z_elems), dtype=jnp.float32)
    along_y = jnp.asarray(np.tile(GAUSS_WEIGHTS, y_elems), dtype=jnp.float32)
    along_x = jnp.asarray(np.tile(GAUSS_WEIGHTS, x_elems), dtype=jnp.float32)
    return along_z[:, None, None] * along_y[None, :, None] * along_x[None, None, :]


def gradients(node_field, tables):
    z_value, z_slope, y_value, y_slope, value_along_x, x_slope = tables
    highest = lax.Precision.HIGHEST
    value_z = jnp.einsum("czyx,zk->ckyx", node_field, z_value, precision=highest)
    slope_z = jnp.einsum("czyx,zk->ckyx", node_field, z_slope, precision=highest)
    value_zy = jnp.einsum("ckyx,yl->cklx", value_z, y_value, precision=highest)
    slope_y = jnp.einsum("ckyx,yl->cklx", value_z, y_slope, precision=highest)
    slope_zy = jnp.einsum("ckyx,yl->cklx", slope_z, y_value, precision=highest)
    deriv_x = jnp.einsum("cklx,xm->cklm", value_zy, x_slope, precision=highest)
    deriv_y = jnp.einsum("cklx,xm->cklm", slope_y, value_along_x, precision=highest)
    deriv_z = jnp.einsum("cklx,xm->cklm", slope_zy, value_along_x, precision=highest)
    return jnp.stack([deriv_x, deriv_y, deriv_z], axis=1)


def identity_block():
    return jnp.eye(3, dtype=jnp.float32)[:, :, None, None, None]


def gram(left_part, right_part):
    return jnp.sum(left_part[:, :, None] * right_part[:, None, :], axis=0)


def energy(node_field, tables, target_size_scale, weights):
    jacobian = gradients(node_field, tables) + identity_block()
    strain = gram(jacobian, jacobian) * target_size_scale - identity_block()
    return jnp.sum(weights * jnp.sum(strain * strain, axis=(0, 1)))


def line_terms(node_field, direction, tables, target_size_scale, weights):
    jacobian = gradients(node_field, tables) + identity_block()
    motion = gradients(direction, tables)
    strain_zero = gram(jacobian, jacobian) * target_size_scale - identity_block()
    mixed = gram(jacobian, motion)
    strain_one = (mixed + jnp.swapaxes(mixed, 0, 1)) * target_size_scale
    strain_two = gram(motion, motion) * target_size_scale

    def weighted(first_part, latter_portion):
        return jnp.sum(weights * jnp.sum(first_part * latter_portion, axis=(0, 1)))

    zero_zero = weighted(strain_zero, strain_zero)
    zero_one = weighted(strain_zero, strain_one)
    zero_two = weighted(strain_zero, strain_two)
    one_two = weighted(strain_one, strain_two)
    two_two = weighted(strain_two, strain_two)
    gauss_newton = weighted(strain_one, strain_one)
    return (
        zero_zero,
        2.0 * zero_one,
        gauss_newton + 2.0 * zero_two,
        2.0 * one_two,
        two_two,
        gauss_newton,
    )


def line_search(terms):
    const_term, linear, quadratic, cubic_term, quartic, gauss_newton = terms
    step_len = jnp.zeros((), jnp.float32)
    for search_turn in range(LS_STEPS):
        slope = linear + step_len * (
            2.0 * quadratic + step_len * (3.0 * cubic_term + step_len * 4.0 * quartic)
        )
        curvature = 2.0 * quadratic + step_len * (6.0 * cubic_term + step_len * 12.0 * quartic)
        step_len = step_len - slope / jnp.maximum(curvature, gauss_newton + 1e-06)
    return step_len


def inverse_square(coefs, coords):
    along_x = coords[:, 0]
    along_y = coords[:, 1]
    along_z = coords[:, 2]
    summed = jnp.zeros_like(along_x)
    for corner in range(8):
        weight_x = along_x if corner & 1 else 1.0 - along_x
        weight_y = along_y if corner & 2 else 1.0 - along_y
        weight_z = along_z if corner & 4 else 1.0 - along_z
        summed = summed + weight_x * weight_y * weight_z * coefs[:, corner]
    return jnp.exp(-2.0 * summed)


def gather_coefs(table, elem_ids):
    index_rows = elem_ids[:, 0, :]
    corner_rows = jnp.take(jnp.transpose(table), index_rows, axis=0)
    return jnp.moveaxis(corner_rows, 2, 1)


def answer(reply):
    return lax.all_to_all(reply, ("mesh", "bg"), split_axis=0, concat_axis=0, tiled=True)


def assemble(local_part):
    padded_z = extended(local_part, (("mesh", 1),), 1)
    partial_sum = local_part.at[:, 0].add(padded_z[:, 0]).at[:, -1].add(padded_z[:, -1])
    padded_y = extended(partial_sum, (("bg", 2),), 1)
    summed = partial_sum.at[:, :, 0].add(padded_y[:, :, 0]).at[:, :, -1].add(padded_y[:, :, -1])
    return summed


def shards(displacement, bg_coef, query_elem, query_point, query_coord):
    devices = lax.axis_size("mesh") * lax.axis_size("bg")
    z_elems = displacement.shape[1] // 2
    y_elems = displacement.shape[2] // 2
    x_elems = displacement.shape[3] // 2
    tables = (
        basis_tables(z_elems, False) + basis_tables(y_elems, False) + basis_tables(x_elems, True)
    )
    weights = quad_weights(z_elems, y_elems, x_elems)
    point_count = 27 * z_elems * y_elems * x_elems
    elem_ids = query_elem.reshape(devices, 1, -1)
    coords = query_coord.reshape(devices, 3, -1)
    fetched = answer(
        gather_coefs(
            bg_coef,
            lax.all_to_all(elem_ids, ("mesh", "bg"), split_axis=0, concat_axis=0, tiled=True),
        )
    )
    found_vals = inverse_square(fetched, coords).reshape(-1)
    target_size_scale = (
        jnp.zeros((point_count,), jnp.float32)
        .at[query_point.reshape(-1)]
        .set(found_vals, mode="drop")
    )
    target_size_scale = target_size_scale.reshape(3 * z_elems, 3 * y_elems, 3 * x_elems)

    def local_energy(values):
        return energy(values, tables, target_size_scale, weights)

    node_field = assemble(jnp.pad(displacement, ((0, 0), (0, 1), (0, 1), (0, 0))))
    history = []
    for newton_pass in range(PASSES):
        direction = -assemble(jax.grad(local_energy)(node_field))
        partial_terms = jnp.stack(
            line_terms(node_field, direction, tables, target_size_scale, weights)
        )
        totals = lax.psum(partial_terms, ("mesh", "bg"))
        step_len = line_search(totals)
        node_field = node_field + step_len * direction
        history.append(totals[:5] / (devices * z_elems * y_elems * x_elems))
    return (node_field[:, :-1, :-1], jnp.stack(history))


def solution(mesh):
    in_specs = (
        P(None, "mesh", "bg", None),
        P(None, ("mesh", "bg")),
        P(("mesh", "bg"), None, None),
        P(("mesh", "bg"), None, None),
        P(("mesh", "bg"), None, None, None),
    )
    out_specs = (P(None, "mesh", "bg", None), P())
    return jax.shard_map(shards, mesh=mesh, in_specs=in_specs, out_specs=out_specs, check_vma=False)
```

profile of v0, /device:TPU:1, one launch (start us, length us, event | category | flops | bytes accessed | tf_op | source)
XLA Modules:
  0.0 415.2 jit_solution(10419066818697922350)
XLA Ops:
  0.7 2.1 collective-permute-start
  2.8 1.6 copy.164
  4.4 10.7 %all-to-all-start = ((s32[128,1,136]{2,1,0:T(1,128)}), s32[128,1,136]{2,1,0:T(1,128)S(1)}, u32[]{:S(2)}, u32[]{:S(2)}) async-start(s32[128,1,136]{2,1,0:T(1,128)} %bitcast.21), calls=%async_computation | async-start | bytes 262144 | tf_op jit(solution)/shard_map/all_to_all | solution.py:167
  15.1 1.0 copy.160
  16.2 0.7 compare_select_fusion.1
  16.9 1.0 fusion.53
  18.0 5.5 %collective-permute-start.1 = (f32[3,1,5,128]{3,1,2,0:T(1,128)S(1)}, f32[3,1,5,128]{3,1,2,0:T(1,128)S(1)}, u32[]{:S(2)}, u32[]{:S(2)}) collective-permute-start(f32[3,1,5,128]{3,1,2,0:T(1,128)S(1)} %get-tuple-element.209), channel_id=1, source_target_pairs={{8,0},{16,8},{24,16},{32,24},{40,32},{48,40},{56,48},{64,56},{72,6... | collective-permute-start | bytes 23048 | tf_op jit(solution)/shard_map/ppermute | solution.py:22
  23.5 0.7 collective-permute-done.1
  24.3 2.4 collective-permute-start.2
  26.8 0.8 collective-permute-done.2
  27.5 2.4 collective-permute-start.3
  29.9 5.3 %copy.167 = f32[8,16384]{0,1:T(8,128)} copy(f32[8,16384]{1,0:T(8,128)S(1)} %copy-done.4) | data formatting | bytes 1048576 | tf_op args[1]
  36.9 0.3 convolution_bitcast_fusion.9
  37.3 0.4 fusion.8
  37.8 61.3 %gather_fusion = f32[17408,8]{1,0:T(8,128)} fusion(f32[16384,8]{1,0:T(8,128)} %bitcast.265, s32[17408]{0:T(1024)S(1)} %broadcast_clamp_fusion), kind=kCustom, calls=%fused_computation | custom fusion | bytes 1183744 | tf_op jit(solution)/shard_map/jit(_take)/gather | solution.py:136
  99.1 6.7 %copy.168 = f32[128,136,8]{1,2,0:T(8,128)S(1)} copy(f32[128,136,8]{2,1,0:T(8,128)} %bitcast.266) | data formatting | bytes 1114112 | tf_op jit(solution)/shard_map/jit(_take)/gather | solution.py:136
  106.1 1.1 select_bitcast_fusion
  107.2 7.9 %all-to-all-start.1 = ((f32[128,8,136]{2,1,0:T(8,128)}), f32[128,8,136]{2,1,0:T(8,128)S(1)}, u32[]{:S(2)}, u32[]{:S(2)}) async-start(f32[128,8,136]{2,1,0:T(8,128)} %select_bitcast_fusion), calls=%async_computation.1 | async-start | bytes 2097152 | tf_op jit(solution)/shard_map/all_to_all | solution.py:141
  115.1 0.3 convolution_bitcast_fusion.10
  115.5 0.3 convolution_bitcast_fusion.11
  115.8 0.4 multiply_reduce_fusion.9
  116.3 17.6 %all-to-all-done.1 = f32[128,8,136]{2,1,0:T(8,128)S(1)} async-done(((f32[128,8,136]{2,1,0:T(8,128)}), f32[128,8,136]{2,1,0:T(8,128)S(1)}, u32[]{:S(2)}, u32[]{:S(2)}) %all-to-all-start.1) | async-done | bytes 557088 | tf_op jit(solution)/shard_map/all_to_all | solution.py:141
  133.9 2.9 slice_reduce_fusion.6
  137.9 64.3 %scatter_custom_fusion = f32[6912]{0:T(1024)S(1)} fusion(s32[17408]{0:T(1024)} %bitcast.268, f32[17408]{0:T(1024)S(1)} %multiply_exponential_fusion, f32[]{:T(128)} %constant.313.clone.1), kind=kCustom, calls=%fused_computation.166 | custom fusion | bytes 28160 | tf_op jit(solution)/shard_map/scatter | solution.py:174
  202.3 0.5 multiply_reduce_fusion.8
  205.1 0.5 collective-permute-start.4
  205.6 5.3 %collective-permute-done.4 = f32[3,1,5,128]{3,1,2,0:T(1,128)S(1)} collective-permute-done((f32[3,1,5,128]{3,1,2,0:T(1,128)S(1)}, f32[3,1,5,128]{3,1,2,0:T(1,128)S(1)}, u32[]{:S(2)}, u32[]{:S(2)}) %collective-permute-start.4) | collective-permute-done | bytes 7712 | tf_op jit(solution)/shard_map/ppermute | solution.py:19
  211.1 2.4 collective-permute-done.5
  213.7 3.6 collective-permute-start.6
  217.3 0.8 collective-permute-done.6
  218.1 3.5 collective-permute-start.7
  221.7 0.8 collective-permute-done.7
  223.5 0.3 convolution_bitcast_fusion.6
  223.8 0.3 convolution_bitcast_fusion.7
  224.2 0.3 convolution_bitcast_fusion.8
  224.5 0.7 multiply_reduce_fusion.5
  225.2 0.4 multiply_reduce_fusion.18
  225.6 0.8 fusion.37
  228.9 2.0 stack.121
  230.9 65.5 %psum.14 = f32[6]{0:T(128)S(1)} all-reduce(f32[6]{0:T(128)S(1)} %stack.121), channel_id=1, replica_groups=mesh['mesh'=16,'bg'=8] {'mesh','bg'}, use_global_device_ids=true, to_apply=%region_18.19 | all-reduce | flops 6 | bytes 48 | tf_op jit(solution)/shard_map/psum | solution.py:188
  296.4 0.7 fusion.60
  308.1 0.3 convolution_bitcast_fusion.3
  308.5 0.3 convolution_bitcast_fusion.4
  308.8 0.3 convolution_bitcast_fusion.5
  309.2 0.4 multiply_reduce_fusion.4
  309.7 0.5 multiply_reduce_fusion.3
  310.8 0.3 convolution_bitcast_fusion.15
  312.5 5.8 %collective-permute-done.8 = f32[3,1,5,128]{3,1,2,0:T(1,128)S(1)} collective-permute-done((f32[3,1,5,128]{3,1,2,0:T(1,128)S(1)}, f32[3,1,5,128]{3,1,2,0:T(1,128)S(1)}, u32[]{:S(2)}, u32[]{:S(2)}) %collective-permute-start.8) | collective-permute-done | bytes 7712 | tf_op jit(solution)/shard_map/ppermute | solution.py:19
  318.5 2.4 collective-permute-done.9
  321.0 1.8 collective-permute-start.10
  322.8 2.2 collective-permute-done.10
  325.1 3.7 collective-permute-start.11
  328.7 0.8 collective-permute-done.11
  330.6 0.3 convolution_bitcast_fusion
  330.9 0.3 convolution_bitcast_fusion.1
  331.3 0.3 convolution_bitcast_fusion.2
  331.6 0.7 multiply_reduce_fusion
  332.3 0.4 multiply_reduce_fusion.12
  332.6 0.8 fusion.43
  336.0 2.0 stack.136
  338.0 65.3 %psum.15 = f32[6]{0:T(128)S(1)} all-reduce(f32[6]{0:T(128)S(1)} %stack.136), channel_id=1, replica_groups=mesh['mesh'=16,'bg'=8] {'mesh','bg'}, use_global_device_ids=true, to_apply=%region_36.37 | all-reduce | flops 6 | bytes 48 | tf_op jit(solution)/shard_map/psum | solution.py:188
  403.3 0.7 fusion.59
  414.0 0.6 copy.210
  414.6 0.6 pad_maximum_fusion.2
  (117 shorter events, 11.3 us)
Async XLA Ops:
  0.6 22.8 %copy-start.7 = (f32[6]{0:T(128)S(1)}, f32[6]{0:T(128)}, u32[]{:S(2)}) copy-start(f32[6]{0:T(128)} %constant.334.clone) | copy-start | bytes 76
  0.6 26.0 %copy-start.6 = (f32[192]{0:T(256)S(1)}, f32[192]{0:T(256)}, u32[]{:S(2)}) copy-start(f32[192]{0:T(256)} %constant.335.clone) | copy-start | bytes 2308
  0.7 17.2 %copy-start.5 = (f32[3,4,4,128]{3,2,1,0:T(4,128)S(1)}, f32[3,4,4,128]{3,2,1,0:T(4,128)}, u32[]{:S(2)}) copy-start(f32[3,4,4,128]{3,2,1,0:T(4,128)} %param.38) | copy-start | bytes 73732
  0.7 29.2 %copy-start.4 = (f32[8,16384]{1,0:T(8,128)S(1)}, f32[8,16384]{1,0:T(8,128)}, u32[]{:S(2)}) copy-start(f32[8,16384]{1,0:T(8,128)} %param.39) | copy-start | bytes 1572868
  0.7 17.2 %collective-permute-start = (f32[3,1,5,128]{3,1,2,0:T(1,128)S(1)}, f32[3,1,5,128]{3,1,2,0:T(1,128)S(1)}, u32[]{:S(2)}, u32[]{:S(2)}) collective-permute-start(f32[3,1,5,128]{3,1,2,0:T(1,128)S(1)} %slice.391), channel_id=1, source_target_pairs={{0,8},{8,16},{16,24},{24,32},{32,40},{40,48},{48,56},{56,64},{64,7... | collective-permute-start | bytes 23048 | tf_op jit(solution)/shard_map/ppermute | solution.py:19
  4.4 32.8 %all-to-all-start = ((s32[128,1,136]{2,1,0:T(1,128)}), s32[128,1,136]{2,1,0:T(1,128)S(1)}, u32[]{:S(2)}, u32[]{:S(2)}) async-start(s32[128,1,136]{2,1,0:T(1,128)} %bitcast.21), calls=%async_computation | async-start | bytes 262144 | tf_op jit(solution)/shard_map/all_to_all | solution.py:167
  18.0 6.2 %collective-permute-start.1 = (f32[3,1,5,128]{3,1,2,0:T(1,128)S(1)}, f32[3,1,5,128]{3,1,2,0:T(1,128)S(1)}, u32[]{:S(2)}, u32[]{:S(2)}) collective-permute-start(f32[3,1,5,128]{3,1,2,0:T(1,128)S(1)} %get-tuple-element.209), channel_id=1, source_target_pairs={{8,0},{16,8},{24,16},{32,24},{40,32},{48,40},{56,48},{64,56},{72,6... | collective-permute-start | bytes 23048 | tf_op jit(solution)/shard_map/ppermute | solution.py:22
  24.3 3.2 collective-permute-start.2
  27.5 8.3 %collective-permute-start.3 = (f32[3,5,1,128]{3,1,2,0:T(8,128)S(1)}, f32[3,5,1,128]{3,1,2,0:T(8,128)S(1)}, u32[]{:S(2)}, u32[]{:S(2)}) collective-permute-start(f32[3,5,1,128]{3,1,2,0:T(8,128)S(1)} %get-tuple-element.207), channel_id=1, source_target_pairs={{1,0},{2,1},{3,2},{4,3},{5,4},{6,5},{7,6},{0,7},{9,8},{10,9},{11,1... | collective-permute-start | bytes 23048 | tf_op jit(solution)/shard_map/ppermute | solution.py:22
  29.9 6.0 %copy-start.3 = (f32[5,6,1,1]{0,1,3,2:T(8,128)S(1)}, f32[5,6,1,1]{0,1,3,2:T(8,128)}, u32[]{:S(2)}) copy-start(f32[5,6,1,1]{0,1,3,2:T(8,128)} %constant.344) | copy-start | bytes 364
  35.2 0.9 copy-start.2
  35.2 1.7 copy-start
  107.2 8.3 %copy-start.1 = (f32[128,192,1,1]{0,1,3,2:T(8,128)S(1)}, f32[128,192,1,1]{0,1,3,2:T(8,128)}, u32[]{:S(2)}) copy-start(f32[128,192,1,1]{0,1,3,2:T(8,128)} %constant.343) | copy-start | bytes 294916
  107.2 26.7 %all-to-all-start.1 = ((f32[128,8,136]{2,1,0:T(8,128)}), f32[128,8,136]{2,1,0:T(8,128)S(1)}, u32[]{:S(2)}, u32[]{:S(2)}) async-start(f32[128,8,136]{2,1,0:T(8,128)} %select_bitcast_fusion), calls=%async_computation.1 | async-start | bytes 2097152 | tf_op jit(solution)/shard_map/all_to_all | solution.py:141
  205.1 5.9 %collective-permute-start.4 = (f32[3,1,5,128]{3,1,2,0:T(1,128)S(1)}, f32[3,1,5,128]{3,1,2,0:T(1,128)S(1)}, u32[]{:S(2)}, u32[]{:S(2)}) collective-permute-start(f32[3,1,5,128]{3,1,2,0:T(1,128)S(1)} %slice.440), channel_id=1, source_target_pairs={{0,8},{8,16},{16,24},{24,32},{32,40},{40,48},{48,56},{56,64},{64,7... | collective-permute-start | bytes 23048 | tf_op jit(solution)/shard_map/ppermute | solution.py:19
  211.0 2.6 collective-permute-start.5
  213.7 4.5 %collective-permute-start.6 = (f32[3,5,1,128]{3,1,2,0:T(8,128)S(1)}, f32[3,5,1,128]{3,1,2,0:T(8,128)S(1)}, u32[]{:S(2)}, u32[]{:S(2)}) collective-permute-start(f32[3,5,1,128]{3,1,2,0:T(8,128)S(1)} %slice.443), channel_id=1, source_target_pairs={{0,1},{1,2},{2,3},{3,4},{4,5},{5,6},{6,7},{7,0},{8,9},{9,10},{10,1... | collective-permute-start | bytes 23048 | tf_op jit(solution)/shard_map/ppermute | solution.py:19
  218.1 4.3 %collective-permute-start.7 = (f32[3,5,1,128]{3,1,2,0:T(8,128)S(1)}, f32[3,5,1,128]{3,1,2,0:T(8,128)S(1)}, u32[]{:S(2)}, u32[]{:S(2)}) collective-permute-start(f32[3,5,1,128]{3,1,2,0:T(8,128)S(1)} %get-tuple-element.203), channel_id=1, source_target_pairs={{1,0},{2,1},{3,2},{4,3},{5,4},{6,5},{7,6},{0,7},{9,8},{10,9},{11,1... | collective-permute-start | bytes 23048 | tf_op jit(solution)/shard_map/ppermute | solution.py:22
  312.4 5.9 %collective-permute-start.8 = (f32[3,1,5,128]{3,1,2,0:T(1,128)S(1)}, f32[3,1,5,128]{3,1,2,0:T(1,128)S(1)}, u32[]{:S(2)}, u32[]{:S(2)}) collective-permute-start(f32[3,1,5,128]{3,1,2,0:T(1,128)S(1)} %slice.446), channel_id=1, source_target_pairs={{0,8},{8,16},{16,24},{24,32},{32,40},{40,48},{48,56},{56,64},{64,7... | collective-permute-start | bytes 23048 | tf_op jit(solution)/shard_map/ppermute | solution.py:19
  318.3 2.6 collective-permute-start.9
  321.0 4.1 collective-permute-start.10
  325.1 4.5 %collective-permute-start.11 = (f32[3,5,1,128]{3,1,2,0:T(8,128)S(1)}, f32[3,5,1,128]{3,1,2,0:T(8,128)S(1)}, u32[]{:S(2)}, u32[]{:S(2)}) collective-permute-start(f32[3,5,1,128]{3,1,2,0:T(8,128)S(1)} %get-tuple-element.199), channel_id=1, source_target_pairs={{1,0},{2,1},{3,2},{4,3},{5,4},{6,5},{7,6},{0,7},{9,8},{10,9},{11,1... | collective-permute-start | bytes 23048 | tf_op jit(solution)/shard_map/ppermute | solution.py:22
where the time goes:
time: 416 us; the launch traced here: 415 us
  local copies, waits for them, and re-layouts  153 us (37%)
  blocking collectives  131 us (31%)
  starting transfers between devices  44.3 us (11%)
  waiting for transfers between devices  39.7 us (10%)
  between operations  26.7 us (6%)
  matrix products  12.1 us (3%)
  other arithmetic  9.06 us (2%)
    psum x2, blocking collectives, shards(): totals = lax.psum(partial_terms, ('mesh', 'bg'))  131 us
    gather x2, local copies, waits for them, and re-layouts, gather_coefs(): corner_rows = jnp.take(jnp.transpose(table), index_rows, axis=0)  68 us
    scatter x1, local copies, waits for them, and re-layouts, shards(): target_size_scale = jnp.zeros((point_count,), jnp.float32).at[query_point...  64.3 us
    all_to_all x1, waiting for transfers between devices, answer(): lax.all_to_all(reply, ('mesh', 'bg'), split_axis=0, concat_axis=0, tiled=...  17.6 us
    ppermute x6, starting transfers between devices, extended(): lax.ppermute(lax.slice_in_dim(block, 0, width, axis=dim), axis, backward)  15.1 us
    ppermute x6, waiting for transfers between devices, extended(): lax.ppermute(lax.slice_in_dim(block, block.shape[dim] - width, None, axis...  15 us
    all_to_all x1, starting transfers between devices, shards(): lax.all_to_all(elem_ids, ('mesh', 'bg'), split_axis=0, concat_axis=0, til...  10.7 us
    ppermute x6, starting transfers between devices, extended(): lax.ppermute(lax.slice_in_dim(block, block.shape[dim] - width, None, axis...  10.6 us
  transfers between devices with their start and end apart: 14, of which 11 were waited for; matrix products, arithmetic and copies ran while one was open for 3% of the time, Pallas kernels for 0%

commit v1 on v0

--- a/solution.py
+++ b/solution.py
@@ -185,7 +185,7 @@
         partial_terms = jnp.stack(
             line_terms(node_field, direction, tables, target_size_scale, weights)
         )
-        totals = lax.psum(partial_terms, ("mesh", "bg"))
+        totals = lax.psum(lax.psum(partial_terms, "mesh"), "bg")
         step_len = line_search(totals)
         node_field = node_field + step_len * direction
         history.append(totals[:5] / (devices * z_elems * y_elems * x_elems))

time: 416 us -> 387 us (0.930)
  blocking collectives: 131 us -> 102 us
    psum x2 -> x4, blocking collectives: 131 us -> 102 us  [shards(): totals = lax.psum(lax.psum(partial_terms, 'mesh'), 'bg')]
where the time goes in v1:
time: 387 us; the launch traced here: 386 us
  local copies, waits for them, and re-layouts  153 us (40%)
  blocking collectives  102 us (26%)
  starting transfers between devices  43.6 us (11%)
  waiting for transfers between devices  40 us (10%)
  between operations  26.7 us (7%)
  matrix products  12.1 us (3%)
  other arithmetic  9.06 us (2%)
    psum x4, blocking collectives, shards(): totals = lax.psum(lax.psum(partial_terms, 'mesh'), 'bg')  102 us
    gather x2, local copies, waits for them, and re-layouts, gather_coefs(): corner_rows = jnp.take(jnp.transpose(table), index_rows, axis=0)  68 us
    scatter x1, local copies, waits for them, and re-layouts, shards(): target_size_scale = jnp.zeros((point_count,), jnp.float32).at[query_point...  64.3 us
    all_to_all x1, waiting for transfers between devices, answer(): lax.all_to_all(reply, ('mesh', 'bg'), split_axis=0, concat_axis=0, tiled=...  17.6 us
    ppermute x6, waiting for transfers between devices, extended(): lax.ppermute(lax.slice_in_dim(block, block.shape[dim] - width, None, axis...  15.2 us
    ppermute x6, starting transfers between devices, extended(): lax.ppermute(lax.slice_in_dim(block, 0, width, axis=dim), axis, backward)  15.1 us
    all_to_all x1, starting transfers between devices, shards(): lax.all_to_all(elem_ids, ('mesh', 'bg'), split_axis=0, concat_axis=0, til...  10.7 us
    ppermute x6, starting transfers between devices, extended(): lax.ppermute(lax.slice_in_dim(block, block.shape[dim] - width, None, axis...  9.86 us
  transfers between devices with their start and end apart: 14, of which 11 were waited for; matrix products, arithmetic and copies ran while one was open for 3% of the time, Pallas kernels for 0%

profile of v1, /device:TPU:1, one launch (start us, length us, event | category | flops | bytes accessed | tf_op | source)
XLA Modules:
  0.0 386.3 jit_solution(14983343973571094124)
XLA Ops:
  0.7 2.1 collective-permute-start
  2.8 1.6 copy.164
  4.4 10.7 %all-to-all-start = ((s32[128,1,136]{2,1,0:T(1,128)}), s32[128,1,136]{2,1,0:T(1,128)S(1)}, u32[]{:S(2)}, u32[]{:S(2)}) async-start(s32[128,1,136]{2,1,0:T(1,128)} %bitcast.21), calls=%async_computation | async-start | bytes 262144 | tf_op jit(solution)/shard_map/all_to_all | solution.py:167
  15.1 1.0 copy.160
  16.2 0.7 compare_select_fusion.1
  16.9 1.0 fusion.53
  18.0 5.5 %collective-permute-start.1 = (f32[3,1,5,128]{3,1,2,0:T(1,128)S(1)}, f32[3,1,5,128]{3,1,2,0:T(1,128)S(1)}, u32[]{:S(2)}, u32[]{:S(2)}) collective-permute-start(f32[3,1,5,128]{3,1,2,0:T(1,128)S(1)} %get-tuple-element.209), channel_id=1, source_target_pairs={{8,0},{16,8},{24,16},{32,24},{40,32},{48,40},{56,48},{64,56},{72,6... | collective-permute-start | bytes 23048 | tf_op jit(solution)/shard_map/ppermute | solution.py:22
  23.5 0.7 collective-permute-done.1
  24.3 2.4 collective-permute-start.2
  26.8 0.8 collective-permute-done.2
  27.5 2.4 collective-permute-start.3
  29.9 5.3 %copy.167 = f32[8,16384]{0,1:T(8,128)} copy(f32[8,16384]{1,0:T(8,128)S(1)} %copy-done.4) | data formatting | bytes 1048576 | tf_op args[1]
  36.9 0.3 convolution_bitcast_fusion.9
  37.3 0.4 fusion.8
  37.8 61.3 %gather_fusion = f32[17408,8]{1,0:T(8,128)} fusion(f32[16384,8]{1,0:T(8,128)} %bitcast.265, s32[17408]{0:T(1024)S(1)} %broadcast_clamp_fusion), kind=kCustom, calls=%fused_computation | custom fusion | bytes 1183744 | tf_op jit(solution)/shard_map/jit(_take)/gather | solution.py:136
  99.1 6.7 %copy.168 = f32[128,136,8]{1,2,0:T(8,128)S(1)} copy(f32[128,136,8]{2,1,0:T(8,128)} %bitcast.266) | data formatting | bytes 1114112 | tf_op jit(solution)/shard_map/jit(_take)/gather | solution.py:136
  106.1 1.1 select_bitcast_fusion
  107.2 7.9 %all-to-all-start.1 = ((f32[128,8,136]{2,1,0:T(8,128)}), f32[128,8,136]{2,1,0:T(8,128)S(1)}, u32[]{:S(2)}, u32[]{:S(2)}) async-start(f32[128,8,136]{2,1,0:T(8,128)} %select_bitcast_fusion), calls=%async_computation.1 | async-start | bytes 2097152 | tf_op jit(solution)/shard_map/all_to_all | solution.py:141
  115.1 0.3 convolution_bitcast_fusion.10
  115.5 0.3 convolution_bitcast_fusion.11
  115.8 0.4 multiply_reduce_fusion.9
  116.3 17.6 %all-to-all-done.1 = f32[128,8,136]{2,1,0:T(8,128)S(1)} async-done(((f32[128,8,136]{2,1,0:T(8,128)}), f32[128,8,136]{2,1,0:T(8,128)S(1)}, u32[]{:S(2)}, u32[]{:S(2)}) %all-to-all-start.1) | async-done | bytes 557088 | tf_op jit(solution)/shard_map/all_to_all | solution.py:141
  133.9 2.9 slice_reduce_fusion.6
  137.9 64.3 %scatter_custom_fusion = f32[6912]{0:T(1024)S(1)} fusion(s32[17408]{0:T(1024)} %bitcast.268, f32[17408]{0:T(1024)S(1)} %multiply_exponential_fusion, f32[]{:T(128)} %constant.313.clone.1), kind=kCustom, calls=%fused_computation.166 | custom fusion | bytes 28160 | tf_op jit(solution)/shard_map/scatter | solution.py:174
  202.3 0.5 multiply_reduce_fusion.8
  205.1 0.5 collective-permute-start.4
  205.6 5.3 %collective-permute-done.4 = f32[3,1,5,128]{3,1,2,0:T(1,128)S(1)} collective-permute-done((f32[3,1,5,128]{3,1,2,0:T(1,128)S(1)}, f32[3,1,5,128]{3,1,2,0:T(1,128)S(1)}, u32[]{:S(2)}, u32[]{:S(2)}) %collective-permute-start.4) | collective-permute-done | bytes 7712 | tf_op jit(solution)/shard_map/ppermute | solution.py:19
  211.1 2.4 collective-permute-done.5
  213.7 3.6 collective-permute-start.6
  217.3 0.8 collective-permute-done.6
  218.1 3.5 collective-permute-start.7
  221.7 0.8 collective-permute-done.7
  223.8 0.3 convolution_bitcast_fusion.7
  224.2 0.3 convolution_bitcast_fusion.8
  224.5 0.7 multiply_reduce_fusion.5
  225.2 0.4 multiply_reduce_fusion.18
  225.6 0.8 fusion.37
  228.9 2.0 stack.121
  230.9 31.5 %psum.28 = f32[6]{0:T(128)S(1)} all-reduce(f32[6]{0:T(128)S(1)} %stack.121), channel_id=1, replica_groups=mesh['mesh'=16,'bg'=8] {'mesh'}, use_global_device_ids=true, to_apply=%region_18.19 | all-reduce | flops 6 | bytes 48 | tf_op jit(solution)/shard_map/psum | solution.py:188
  262.4 19.8 %psum.29 = f32[6]{0:T(128)S(1)} all-reduce(f32[6]{0:T(128)S(1)} %psum.28), channel_id=1, replica_groups=mesh['mesh'=16,'bg'=8] {'bg'}, use_global_device_ids=true, to_apply=%region_19.20 | all-reduce | flops 6 | bytes 48 | tf_op jit(solution)/shard_map/psum | solution.py:188
  282.2 0.7 fusion.60
  293.9 0.3 convolution_bitcast_fusion.3
  294.3 0.3 convolution_bitcast_fusion.4
  294.6 0.3 convolution_bitcast_fusion.5
  295.0 0.4 multiply_reduce_fusion.4
  295.5 0.5 multiply_reduce_fusion.3
  298.3 5.8 %collective-permute-done.8 = f32[3,1,5,128]{3,1,2,0:T(1,128)S(1)} collective-permute-done((f32[3,1,5,128]{3,1,2,0:T(1,128)S(1)}, f32[3,1,5,128]{3,1,2,0:T(1,128)S(1)}, u32[]{:S(2)}, u32[]{:S(2)}) %collective-permute-start.8) | collective-permute-done | bytes 7712 | tf_op jit(solution)/shard_map/ppermute | solution.py:19
  304.3 2.4 collective-permute-done.9
  306.8 1.1 collective-permute-start.10
  307.9 2.5 collective-permute-done.10
  310.4 3.7 collective-permute-start.11
  314.1 0.8 collective-permute-done.11
  315.9 0.3 convolution_bitcast_fusion
  316.3 0.3 convolution_bitcast_fusion.1
  316.6 0.3 convolution_bitcast_fusion.2
  317.0 0.7 multiply_reduce_fusion
  317.6 0.4 multiply_reduce_fusion.12
  318.0 0.8 fusion.43
  321.4 2.0 stack.136
  323.4 31.5 %psum.30 = f32[6]{0:T(128)S(1)} all-reduce(f32[6]{0:T(128)S(1)} %stack.136), channel_id=1, replica_groups=mesh['mesh'=16,'bg'=8] {'mesh'}, use_global_device_ids=true, to_apply=%region_37.38 | all-reduce | flops 6 | bytes 48 | tf_op jit(solution)/shard_map/psum | solution.py:188
  354.9 19.6 %psum.31 = f32[6]{0:T(128)S(1)} all-reduce(f32[6]{0:T(128)S(1)} %psum.30), channel_id=1, replica_groups=mesh['mesh'=16,'bg'=8] {'bg'}, use_global_device_ids=true, to_apply=%region_38.39 | all-reduce | flops 6 | bytes 48 | tf_op jit(solution)/shard_map/psum | solution.py:188
  374.5 0.7 fusion.59
  385.2 0.6 copy.210
  385.8 0.6 pad_maximum_fusion.2
  (119 shorter events, 11.9 us)
Async XLA Ops:
  0.6 22.8 %copy-start.7 = (f32[6]{0:T(128)S(1)}, f32[6]{0:T(128)}, u32[]{:S(2)}) copy-start(f32[6]{0:T(128)} %constant.334.clone) | copy-start | bytes 76
  0.6 26.0 %copy-start.6 = (f32[192]{0:T(256)S(1)}, f32[192]{0:T(256)}, u32[]{:S(2)}) copy-start(f32[192]{0:T(256)} %constant.335.clone) | copy-start | bytes 2308
  0.7 17.2 %copy-start.5 = (f32[3,4,4,128]{3,2,1,0:T(4,128)S(1)}, f32[3,4,4,128]{3,2,1,0:T(4,128)}, u32[]{:S(2)}) copy-start(f32[3,4,4,128]{3,2,1,0:T(4,128)} %param.38) | copy-start | bytes 73732
  0.7 29.2 %copy-start.4 = (f32[8,16384]{1,0:T(8,128)S(1)}, f32[8,16384]{1,0:T(8,128)}, u32[]{:S(2)}) copy-start(f32[8,16384]{1,0:T(8,128)} %param.39) | copy-start | bytes 1572868
  0.7 17.2 %collective-permute-start = (f32[3,1,5,128]{3,1,2,0:T(1,128)S(1)}, f32[3,1,5,128]{3,1,2,0:T(1,128)S(1)}, u32[]{:S(2)}, u32[]{:S(2)}) collective-permute-start(f32[3,1,5,128]{3,1,2,0:T(1,128)S(1)} %slice.391), channel_id=1, source_target_pairs={{0,8},{8,16},{16,24},{24,32},{32,40},{40,48},{48,56},{56,64},{64,7... | collective-permute-start | bytes 23048 | tf_op jit(solution)/shard_map/ppermute | solution.py:19
  4.4 32.8 %all-to-all-start = ((s32[128,1,136]{2,1,0:T(1,128)}), s32[128,1,136]{2,1,0:T(1,128)S(1)}, u32[]{:S(2)}, u32[]{:S(2)}) async-start(s32[128,1,136]{2,1,0:T(1,128)} %bitcast.21), calls=%async_computation | async-start | bytes 262144 | tf_op jit(solution)/shard_map/all_to_all | solution.py:167
  18.0 6.2 %collective-permute-start.1 = (f32[3,1,5,128]{3,1,2,0:T(1,128)S(1)}, f32[3,1,5,128]{3,1,2,0:T(1,128)S(1)}, u32[]{:S(2)}, u32[]{:S(2)}) collective-permute-start(f32[3,1,5,128]{3,1,2,0:T(1,128)S(1)} %get-tuple-element.209), channel_id=1, source_target_pairs={{8,0},{16,8},{24,16},{32,24},{40,32},{48,40},{56,48},{64,56},{72,6... | collective-permute-start | bytes 23048 | tf_op jit(solution)/shard_map/ppermute | solution.py:22
  24.3 3.2 collective-permute-start.2
  27.5 8.3 %collective-permute-start.3 = (f32[3,5,1,128]{3,1,2,0:T(8,128)S(1)}, f32[3,5,1,128]{3,1,2,0:T(8,128)S(1)}, u32[]{:S(2)}, u32[]{:S(2)}) collective-permute-start(f32[3,5,1,128]{3,1,2,0:T(8,128)S(1)} %get-tuple-element.207), channel_id=1, source_target_pairs={{1,0},{2,1},{3,2},{4,3},{5,4},{6,5},{7,6},{0,7},{9,8},{10,9},{11,1... | collective-permute-start | bytes 23048 | tf_op jit(solution)/shard_map/ppermute | solution.py:22
  29.9 6.0 %copy-start.3 = (f32[5,6,1,1]{0,1,3,2:T(8,128)S(1)}, f32[5,6,1,1]{0,1,3,2:T(8,128)}, u32[]{:S(2)}) copy-start(f32[5,6,1,1]{0,1,3,2:T(8,128)} %constant.344) | copy-start | bytes 364
  35.2 0.9 copy-start.2
  35.2 1.7 copy-start
  107.2 8.3 %copy-start.1 = (f32[128,192,1,1]{0,1,3,2:T(8,128)S(1)}, f32[128,192,1,1]{0,1,3,2:T(8,128)}, u32[]{:S(2)}) copy-start(f32[128,192,1,1]{0,1,3,2:T(8,128)} %constant.343) | copy-start | bytes 294916
  107.2 26.7 %all-to-all-start.1 = ((f32[128,8,136]{2,1,0:T(8,128)}), f32[128,8,136]{2,1,0:T(8,128)S(1)}, u32[]{:S(2)}, u32[]{:S(2)}) async-start(f32[128,8,136]{2,1,0:T(8,128)} %select_bitcast_fusion), calls=%async_computation.1 | async-start | bytes 2097152 | tf_op jit(solution)/shard_map/all_to_all | solution.py:141
  205.1 5.9 %collective-permute-start.4 = (f32[3,1,5,128]{3,1,2,0:T(1,128)S(1)}, f32[3,1,5,128]{3,1,2,0:T(1,128)S(1)}, u32[]{:S(2)}, u32[]{:S(2)}) collective-permute-start(f32[3,1,5,128]{3,1,2,0:T(1,128)S(1)} %slice.440), channel_id=1, source_target_pairs={{0,8},{8,16},{16,24},{24,32},{32,40},{40,48},{48,56},{56,64},{64,7... | collective-permute-start | bytes 23048 | tf_op jit(solution)/shard_map/ppermute | solution.py:19
  211.0 2.6 collective-permute-start.5
  213.7 4.5 %collective-permute-start.6 = (f32[3,5,1,128]{3,1,2,0:T(8,128)S(1)}, f32[3,5,1,128]{3,1,2,0:T(8,128)S(1)}, u32[]{:S(2)}, u32[]{:S(2)}) collective-permute-start(f32[3,5,1,128]{3,1,2,0:T(8,128)S(1)} %slice.443), channel_id=1, source_target_pairs={{0,1},{1,2},{2,3},{3,4},{4,5},{5,6},{6,7},{7,0},{8,9},{9,10},{10,1... | collective-permute-start | bytes 23048 | tf_op jit(solution)/shard_map/ppermute | solution.py:19
  218.1 4.3 %collective-permute-start.7 = (f32[3,5,1,128]{3,1,2,0:T(8,128)S(1)}, f32[3,5,1,128]{3,1,2,0:T(8,128)S(1)}, u32[]{:S(2)}, u32[]{:S(2)}) collective-permute-start(f32[3,5,1,128]{3,1,2,0:T(8,128)S(1)} %get-tuple-element.203), channel_id=1, source_target_pairs={{1,0},{2,1},{3,2},{4,3},{5,4},{6,5},{7,6},{0,7},{9,8},{10,9},{11,1... | collective-permute-start | bytes 23048 | tf_op jit(solution)/shard_map/ppermute | solution.py:22
  298.3 5.9 %collective-permute-start.8 = (f32[3,1,5,128]{3,1,2,0:T(1,128)S(1)}, f32[3,1,5,128]{3,1,2,0:T(1,128)S(1)}, u32[]{:S(2)}, u32[]{:S(2)}) collective-permute-start(f32[3,1,5,128]{3,1,2,0:T(1,128)S(1)} %slice.446), channel_id=1, source_target_pairs={{0,8},{8,16},{16,24},{24,32},{32,40},{40,48},{48,56},{56,64},{64,7... | collective-permute-start | bytes 23048 | tf_op jit(solution)/shard_map/ppermute | solution.py:19
  304.2 2.6 collective-permute-start.9
  306.8 3.6 collective-permute-start.10
  310.4 4.5 %collective-permute-start.11 = (f32[3,5,1,128]{3,1,2,0:T(8,128)S(1)}, f32[3,5,1,128]{3,1,2,0:T(8,128)S(1)}, u32[]{:S(2)}, u32[]{:S(2)}) collective-permute-start(f32[3,5,1,128]{3,1,2,0:T(8,128)S(1)} %get-tuple-element.199), channel_id=1, source_target_pairs={{1,0},{2,1},{3,2},{4,3},{5,4},{6,5},{7,6},{0,7},{9,8},{10,9},{11,1... | collective-permute-start | bytes 23048 | tf_op jit(solution)/shard_map/ppermute | solution.py:22
